TPU v7x, 32 devices: a whole 2x2x4 slice. The times are simulated.
32 devices in a mesh: section: 2 (over core), dp: 16 (over z, y, x).
Axes of the slice: x: 2, y: 2, z: 4, core: 2. Of those that a mesh axis runs over, the one named last changes fastest.
Arguments:
- inputs: bfloat16 [2, 16, 256, 768], P(None, 'dp'), may hold values from -6 to 6
- cotangent: bfloat16 [2, 16, 256, 768], P(None, 'dp'), may hold values from -6 to 6
- lengths: int32 [2, 16], P(None, 'dp'), may hold values from 64 to 256, as said below
- w_query: bfloat16 [2, 768, 768], P('section'), may hold values from -0.21875 to 0.21875
- w_key: bfloat16 [2, 768, 768], P('section'), may hold values from -0.21875 to 0.21875
- w_value: bfloat16 [2, 768, 768], P('section'), may hold values from -0.21875 to 0.21875
- w_output: bfloat16 [2, 768, 768], P('section'), may hold values from -1.75 to 1.75
- w_in: bfloat16 [2, 768, 3072], P('section'), may hold values from -0.21875 to 0.21875
- w_out: bfloat16 [2, 3072, 768], P('section'), may hold values from -0.109375 to 0.109375
- gain_attn: float32 [2, 768], P('section'), may hold values from 0.5 to 1.5
- gain_ffn: float32 [2, 768], P('section'), may hold values from 0.5 to 1.5
- mix_pre: float32 [2, 12, 12], P('section'), may hold values from -1.75 to 1.75
- mix_post: float32 [2, 12, 12], P('section'), may hold values from -1.75 to 1.75
Outputs:
- layer_outputs: bfloat16 [2, 2, 16, 256, 768], P('section', None, 'dp')
- input_grads: bfloat16 [2, 2, 16, 256, 768], P('section', None, 'dp')
- grad_query: float32 [2, 768, 768], P('section')
- grad_key: float32 [2, 768, 768], P('section')
- grad_value: float32 [2, 768, 768], P('section')
- grad_output: float32 [2, 768, 768], P('section')
- grad_in: float32 [2, 768, 3072], P('section')
- grad_out: float32 [2, 3072, 768], P('section')
- grad_gain_attn: float32 [2, 768], P('section')
- grad_gain_ffn: float32 [2, 768], P('section')
- grad_mix_pre: float32 [2, 12, 12], P('section')
- grad_mix_post: float32 [2, 12, 12], P('section')
- rms_stats: float32 [2, 3], P('section')
Inputs may be any that keep to these rules, and one draw needn't show every extreme that they name: Sequence s of micro-batch m holds valid tokens at positions 0 to lengths[m, s] - 1 of its padded row; some sequence has length 256 and some has length 64.
All inputs are finite; a program needn't handle non-finite values.
Results may differ from a plain program's by a relative error of at most 0.018.
Values may be sent and summed in bfloat16 or wider, within the bound.
No kernel may reach another device: no remote copies, remote signals or barrier semaphores. Data moves between devices by JAX's collectives and lax.ppermute only.
A program may use at most 256 MiB of HBM per device.

v0:
```python
import jax
import jax.numpy as jnp
from jax import lax
from jax.sharding import PartitionSpec as P

EPSILON = 1e-06
MASKED = -1e30
F32 = jnp.float32
BF16 = jnp.bfloat16


def dot(a, b, dims):
    return lax.dot_general(a, b, ((dims[0], dims[1]), ((), ())), preferred_element_type=F32)


def mix_heads(mix, values):
    return jnp.einsum("gh,hij->gij", mix, values, precision=lax.Precision.HIGH)


def norm_scale(values):
    return lax.rsqrt(jnp.mean(values * values, axis=-1, keepdims=True) + EPSILON)


def norm_back(values, gain, grad):
    scale = norm_scale(values)
    weighted = grad * gain
    inner = jnp.mean(values * weighted, axis=-1, keepdims=True)
    grad_values = scale * weighted - values * (scale * scale * scale) * inner
    grad_gain = jnp.sum(grad * values * scale, axis=0)
    return (grad_values, grad_gain)


def gelu_pair(values):
    inner = 0.7978845608028654 * (values + 0.044715 * values * values * values)
    tanh = jnp.tanh(inner)
    value = 0.5 * values * (1.0 + tanh)
    slope = 0.5 * (1.0 + tanh) + 0.5 * values * (1.0 - tanh * tanh) * (
        0.7978845608028654 * (1.0 + 3.0 * 0.044715 * values * values)
    )
    return (value, slope)


def forward(values, valid, params):
    w_query, w_key, w_value, w_output, w_in, w_out, gain_attn, gain_ffn, mix_pre, mix_post = params
    length, width = values.shape
    heads = mix_pre.shape[0]
    split = (length, heads, width // heads)
    normed = (values * norm_scale(values) * gain_attn).astype(BF16)
    query = dot(normed, w_query, ((1,), (0,))).astype(BF16).reshape(split)
    key = dot(normed, w_key, ((1,), (0,))).astype(BF16).reshape(split)
    value = dot(normed, w_value, ((1,), (0,))).astype(BF16).reshape(split)
    scores = jnp.einsum("ihd,jhd->hij", query, key, preferred_element_type=F32) * split[2] ** (-0.5)
    rows = lax.broadcasted_iota(jnp.int32, (length, length), 0)
    columns = lax.broadcasted_iota(jnp.int32, (length, length), 1)
    logits = jnp.where(columns <= rows, mix_heads(mix_pre, scores), MASKED)
    exponent = jnp.exp(logits - jnp.max(logits, axis=-1, keepdims=True))
    probs = exponent / jnp.sum(exponent, axis=-1, keepdims=True)
    weights = mix_heads(mix_post, probs).astype(BF16)
    head_out = jnp.einsum("hij,jhd->ihd", weights, value, preferred_element_type=F32)
    head_out = head_out.astype(BF16).reshape(length, width)
    branch_attn = dot(head_out, w_output, ((1,), (0,)))
    residual = values + branch_attn
    normed_ffn = (residual * norm_scale(residual) * gain_ffn).astype(BF16)
    pre_act = dot(normed_ffn, w_in, ((1,), (0,)))
    activation, slope = gelu_pair(pre_act)
    activation = activation.astype(BF16)
    branch_ffn = dot(activation, w_out, ((1,), (0,)))
    out = valid * (residual + branch_ffn)
    squares = jnp.stack(
        [
            jnp.sum(jnp.mean(out * out, axis=-1)),
            jnp.sum(valid[:, 0] * jnp.mean(branch_attn * branch_attn, axis=-1)),
            jnp.sum(valid[:, 0] * jnp.mean(branch_ffn * branch_ffn, axis=-1)),
        ]
    )
    saved = (
        normed,
        query,
        key,
        value,
        scores,
        probs,
        weights,
        head_out,
        residual,
        normed_ffn,
        activation,
        slope,
    )
    return (out.astype(BF16), squares, saved)


def backward_ffn(grad_sum, params, saved):
    w_in, w_out, gain_ffn = (params[4], params[5], params[7])
    residual, normed_ffn, activation, slope = saved[8:]
    grad_branch = grad_sum.astype(BF16)
    grad_act = dot(grad_branch, w_out, ((1,), (1,)))
    grad_pre = (grad_act * slope).astype(BF16)
    grad_normed = dot(grad_pre, w_in, ((1,), (1,)))
    back, grad_gain = norm_back(residual, gain_ffn, grad_normed)
    return (grad_sum + back, grad_gain, (activation, grad_branch, normed_ffn, grad_pre))


def backward_attention(values, grad_resid, params, saved):
    w_query, w_key, w_value, w_output = params[:4]
    gain_attn, mix_pre, mix_post = (params[6], params[8], params[9])
    normed, query, key, value, scores, probs, weights, head_out = saved[:8]
    length, heads, size = query.shape
    grad_attn = grad_resid.astype(BF16)
    grad_heads = dot(grad_attn, w_output, ((1,), (1,))).astype(BF16).reshape(query.shape)
    grad_weights = jnp.einsum("ihd,jhd->hij", grad_heads, value, preferred_element_type=F32)
    grad_value = jnp.einsum("hij,ihd->jhd", weights, grad_heads, preferred_element_type=F32)
    grad_mix_post = jnp.einsum("gij,hij->gh", grad_weights, probs, precision=lax.Precision.HIGH)
    grad_probs = mix_heads(mix_post.T, grad_weights)
    grad_logits = probs * (grad_probs - jnp.sum(probs * grad_probs, axis=-1, keepdims=True))
    grad_mix_pre = jnp.einsum("gij,hij->gh", grad_logits, scores, precision=lax.Precision.HIGH)
    grad_scores = mix_heads(mix_pre.T, grad_logits).astype(BF16)
    scale = size ** (-0.5)
    grad_query = jnp.einsum("hij,jhd->ihd", grad_scores, key, preferred_element_type=F32) * scale
    grad_key = jnp.einsum("hij,ihd->jhd", grad_scores, query, preferred_element_type=F32) * scale
    width = heads * size
    pieces = tuple(
        (piece.astype(BF16).reshape(length, width) for piece in (grad_query, grad_key, grad_value))
    )
    grad_normed = sum(
        (
            dot(piece, matrix, ((1,), (1,)))
            for piece, matrix in zip(pieces, (w_query, w_key, w_value))
        )
    )
    back, grad_gain = norm_back(values, gain_attn, grad_normed)
    return (
        grad_resid + back,
        grad_gain,
        grad_mix_pre,
        grad_mix_post,
        (normed, head_out, grad_attn) + pieces,
    )


def local(
    inputs,
    cotangent,
    lengths,
    w_query,
    w_key,
    w_value,
    w_output,
    w_in,
    w_out,
    gain_attn,
    gain_ffn,
    mix_pre,
    mix_post,
):
    core = lax.axis_index("section")
    is_first = core == 0
    swap = lambda shard: lax.ppermute(shard, "section", [(0, 1), (1, 0)])
    length, width = inputs.shape[2:]
    hidden = w_in.shape[2]
    own = (w_query, w_key, w_value, w_output, w_in, w_out, gain_attn, gain_ffn, mix_pre, mix_post)
    other = tuple((swap(weight) for weight in own))
    layers = (
        tuple((jnp.where(is_first, a, b)[0] for a, b in zip(own, other))),
        tuple((jnp.where(is_first, b, a)[0] for a, b in zip(own, other))),
    )
    take = lambda whole: lax.dynamic_index_in_dim(whole, core, 0, keepdims=False)[0]
    values = take(inputs).astype(F32)
    upstream = take(cotangent).astype(F32)
    valid = (lax.broadcasted_iota(jnp.int32, (length, 1), 0) < take(lengths)).astype(F32)
    outputs, squares, kept, starts = ([], [], [], [])
    layer_in = values
    for params in layers:
        starts.append(layer_in)
        rounded, square, saved = forward(layer_in, valid, params)
        outputs.append(rounded)
        squares.append(square)
        kept.append(saved)
        layer_in = rounded.astype(F32)

    def split_cols(array):
        half = array.shape[1] // 2
        mine = lax.dynamic_slice_in_dim(array, core * half, half, 1)
        theirs = lax.dynamic_slice_in_dim(array, (1 - core) * half, half, 1)
        return (mine, theirs)

    def both_rows(array):
        return jnp.concatenate([array, swap(array)], axis=0)

    def both_half(array):
        mine, theirs = split_cols(array)
        return jnp.concatenate([mine, swap(theirs)], axis=0)

    def weight_grad(left, right):
        return dot(left, right, ((0,), (0,))).astype(BF16)

    grads = [None, None]
    small = [None, None]
    input_grads = [None, None]
    for index in (1, 0):
        params, saved = (layers[index], kept[index])
        grad_sum = valid * upstream
        grad_resid, gain_ffn_grad, ffn = backward_ffn(grad_sum, params, saved)
        activation, grad_branch, normed_ffn, grad_pre = ffn
        down = weight_grad(both_half(activation), both_rows(grad_branch))
        up = weight_grad(both_rows(normed_ffn), both_half(grad_pre))
        grad_in, gain_attn_grad, mix_pre_grad, mix_post_grad, attn = backward_attention(
            starts[index], grad_resid, params, saved
        )
        normed, head_out, grad_attn, grad_query, grad_key, grad_value = attn
        rows = both_rows(normed)
        sides = [
            weight_grad(rows, both_half(piece)) for piece in (grad_query, grad_key, grad_value)
        ]
        sides.append(weight_grad(both_rows(head_out), both_half(grad_attn)))
        blocks = [down]
        blocks += [up[:, at * width : (at + 1) * width] for at in range(up.shape[1] // width)]
        blocks += [jnp.concatenate(sides[:2], axis=1), jnp.concatenate(sides[2:], axis=1)]
        grads[index] = jnp.concatenate(blocks, axis=0)
        small[index] = jnp.concatenate(
            [
                gain_attn_grad,
                gain_ffn_grad,
                mix_pre_grad.reshape(-1),
                mix_post_grad.reshape(-1),
                squares[index],
            ]
        )
        input_grads[index] = grad_in.astype(BF16)
        upstream = input_grads[index].astype(F32)
    shards = [lax.psum_scatter(grad, "dp", scatter_dimension=0, tiled=True) for grad in grads]
    mine = jnp.where(is_first, shards[0], shards[1])
    theirs = swap(jnp.where(is_first, shards[1], shards[0]))
    halves = jnp.concatenate(
        [jnp.where(is_first, mine, theirs), jnp.where(is_first, theirs, mine)], axis=0
    )
    whole = lax.all_gather(halves, "dp", axis=0)
    ranks = whole.shape[0]
    whole = (
        whole.reshape(ranks, 2, -1, width).transpose(1, 0, 2, 3).reshape(2, -1, width).astype(F32)
    )
    half = width // 2
    count = hidden // 2
    w_out_grad = whole[:, :count].reshape(1, hidden, width)
    blocks = hidden // 2 // width
    up = whole[:, count : count + blocks * width].reshape(2 * blocks, width, width)
    w_in_grad = up.transpose(1, 0, 2).reshape(1, width, hidden)
    rest = whole[:, count + blocks * width :].reshape(2, 2, width, 2, half)
    rest = rest.transpose(1, 3, 2, 0, 4).reshape(4, 1, width, width)
    both = jnp.stack(small)
    total_small = jnp.where(is_first, both, both[::-1])
    mine_small = total_small[0] + swap(total_small[1])
    tail = jnp.concatenate([mine_small, jnp.sum(valid)[None] + swap(jnp.sum(valid)[None])])
    tail = lax.psum(tail, "dp")
    heads = mix_pre.shape[1]
    square = heads * heads
    at = 2 * width
    rms = jnp.sqrt(tail[at + 2 * square : at + 2 * square + 3] / tail[-1])[None]

    def place(pair):
        mine = jnp.where(is_first, pair[0], pair[1])
        theirs = swap(jnp.where(is_first, pair[1], pair[0]))
        ordered = [jnp.where(is_first, mine, theirs), jnp.where(is_first, theirs, mine)]
        return jnp.stack(ordered)[None, :, None]

    return (
        place(outputs),
        place(input_grads),
        rest[0],
        rest[1],
        rest[2],
        rest[3],
        w_in_grad,
        w_out_grad,
        tail[None, :width],
        tail[None, width:at],
        tail[at : at + square].reshape(1, heads, heads),
        tail[at + square : at + 2 * square].reshape(1, heads, heads),
        rms,
    )


def solution(mesh):
    in_specs = (
        P(None, "dp", None, None),
        P(None, "dp", None, None),
        P(None, "dp"),
        P("section", None, None),
        P("section", None, None),
        P("section", None, None),
        P("section", None, None),
        P("section", None, None),
        P("section", None, None),
        P("section", None),
        P("section", None),
        P("section", None, None),
        P("section", None, None),
    )
    out_specs = (
        P("section", None, "dp", None, None),
        P("section", None, "dp", None, None),
        P("section", None, None),
        P("section", None, None),
        P("section", None, None),
        P("section", None, None),
        P("section", None, None),
        P("section", None, None),
        P("section", None),
        P("section", None),
        P("section", None, None),
        P("section", None, None),
        P("section", None),
    )
    return jax.shard_map(local, mesh=mesh, in_specs=in_specs, out_specs=out_specs, check_vma=False)
```

profile of v0, /device:TPU:0, one launch (start us, length us, event | category | flops | bytes accessed | tf_op | source)
XLA Modules:
  0.0 790.0 jit_solution(18255932944527995268)
XLA Ops:
  13.1 6.0 collective-permute-done.2
  28.9 3.0 convolution_convert_fusion.22
  38.2 4.2 select_reduce_fusion.1
  42.4 2.1 copy-done.4
  47.4 4.8 fusion.204
  54.6 2.3 multiply_reduce_fusion.13
  57.7 6.3 multiply_convert_fusion.1
  64.0 2.5 fusion.138
  76.6 4.2 select_reduce_fusion
  80.8 2.2 fusion.47
  83.0 3.1 fusion.199
  86.9 2.7 multiply_reduce_fusion.12
  89.9 4.2 multiply_convert_fusion
  94.2 5.9 fusion.38
  100.0 5.2 multiply_reduce_fusion.5
  105.3 5.8 fusion.246
  111.8 2.6 convolution_convert_fusion.15
  116.4 2.5 convolution_convert_fusion.14
  120.8 6.9 multiply_reduce_fusion.1
  127.8 4.3 fusion.74
  133.5 2.1 fusion.90
  139.6 3.1 fusion.41
  144.7 2.5 multiply_reduce_fusion.6
  152.4 2.5 convolution_convert_fusion.12
  156.7 6.7 multiply_reduce_fusion
  163.5 4.3 fusion.75
  171.4 2.1 fusion.131
  182.6 2.8 fusion.49
  203.0 2.8 fusion.48
  210.3 132.8 %reduce-scatter.3.cloned.1.call-done = bf16[288,768]{1,0:T(8,128)(2,1)} async-done(((bf16[4608,768]{1,0:T(8,128)(2,1)}), bf16[288,768]{1,0:T(8,128)(2,1)}) %reduce-scatter.3.cloned.1.call-update) | async-done | bytes 442384 | tf_op jit(solution)/shard_map/reduce_scatter | solution.py:231
  343.1 155.2 %reduce-scatter.5.cloned.1.call-done = bf16[288,768]{1,0:T(8,128)(2,1)} async-done(((bf16[4608,768]{1,0:T(8,128)(2,1)}), bf16[288,768]{1,0:T(8,128)(2,1)}) %reduce-scatter.5.cloned.1.call-update) | async-done | bytes 442384 | tf_op jit(solution)/shard_map/reduce_scatter | solution.py:231
  510.3 9.0 %fusion.104 = f32[12,12]{1,0:T(8,128)} fusion(f32[12,256,256]{2,1,0:T(8,128)} %copy-done.30, f32[12,256,256]{2,0,1:T(8,128)} %copy-done.6, f32[12,256]{0,1:T(8,128)} %copy-done.83, f32[12,256]{0,1:T(8,128)} %copy-done.68, pred[256,256]{1,0:T(8,128)(4,1)} %iota_compare_fusion), kind=kOutput, calls=%fused_computation.176 | convolution fusion | flops 58982400 | bytes 6382144 | tf_op jit(solution)/shard_map/gij,hij->gh/dot_general | solution.py:113
  520.6 10.1 %fusion.113 = f32[12,12]{1,0:T(8,128)} fusion(f32[12,256,256]{2,1,0:T(8,128)S(1)} %convolution_multiply_fusion, f32[12,256,256]{2,0,1:T(8,128)} %copy-done.118, f32[12,256]{0,1:T(8,128)} %copy-done.120, f32[12,256,256]{2,0,1:T(8,128)} %copy-done.6, f32[12,256]{0,1:T(8,128)} %copy-done.83, f32[12,256]{0,1:T(8,128)} %copy-done.68, ...), kind=kOutput, calls=%fused_computation.179 | convolution fusion | flops 60555264 | bytes 9540160 | tf_op jit(solution)/shard_map/gij,hij->gh/dot_general | solution.py:116
  536.5 2.7 concatenate.118
  539.2 8.8 %fusion.107 = f32[12,12]{1,0:T(8,128)} fusion(f32[12,256,256]{2,1,0:T(8,128)} %copy-done.31, f32[12,256,256]{2,0,1:T(8,128)} %copy-done.4, f32[12,256]{0,1:T(8,128)} %copy-done.81, f32[12,256]{0,1:T(8,128)} %copy-done.66, pred[256,256]{1,0:T(8,128)(4,1)} %iota_compare_fusion), kind=kOutput, calls=%fused_computation.177 | convolution fusion | flops 58982400 | bytes 6382144 | tf_op jit(solution)/shard_map/gij,hij->gh/dot_general | solution.py:113
  549.3 9.7 %fusion.110 = f32[12,12]{1,0:T(8,128)} fusion(f32[12,256,256]{2,1,0:T(8,128)S(1)} %copy-done.3, f32[12,256,256]{2,0,1:T(8,128)} %copy-done.119, f32[12,256]{0,1:T(8,128)} %copy-done.121, f32[12,256,256]{2,0,1:T(8,128)} %copy-done.4, f32[12,256]{0,1:T(8,128)} %copy-done.81, f32[12,256]{0,1:T(8,128)} %copy-done.66, pred[256,256]{1,0:T(8,128)(4,1)} %iota_compare_fusion), kind=kOutput, calls=%fused_computation.178 | convolution fusion | flops 60555264 | bytes 9540160 | tf_op jit(solution)/shard_map/gij,hij->gh/dot_general | solution.py:116
  563.0 2.7 concatenate.117
  567.4 2.1 broadcast_select_fusion.40
  569.7 42.1 %psum.7 = f32[1828]{0:T(1024)S(1)} all-reduce(f32[1828]{0:T(1024)S(1)} %pad_maximum_fusion.10), channel_id=1, replica_groups=mesh['section'=2,'dp'=16] {'dp'}, use_global_device_ids=true, to_apply=%region_33.34 | all-reduce | flops 1828 | bytes 14624 | tf_op jit(solution)/shard_map/psum | solution.py:254
  619.4 51.2 %all-gather.3.cloned.1.call-done = bf16[9216,768]{1,0:T(8,128)(2,1)} async-done(((bf16[576,768]{1,0:T(8,128)(2,1)}), bf16[9216,768]{1,0:T(8,128)(2,1)}) %all-gather.3.cloned.1.call-update) | async-done | bytes 14155792 | tf_op jit(solution)/shard_map/all_gather | solution.py:237
  670.6 15.8 %copy.184 = f32[16,2,288,768]{3,2,0,1:T(8,128)} copy(bf16[16,2,288,768]{3,2,1,0:T(8,128)(2,1)} %bitcast.301) | data formatting | bytes 42467328 | tf_op jit(solution)/shard_map/convert_element_type | solution.py:240
  686.4 20.8 %fusion.250 = (f32[2,1536,768]{2,1,0:T(8,128)}, f32[2,1536,768]{2,1,0:T(8,128)}, f32[2,1536,768]{2,1,0:T(8,128)}) fusion(f32[2,4608,768]{2,1,0:T(8,128)} %bitcast.298), kind=kLoop, calls=%fused_computation.396 | loop fusion | bytes 56623104 | tf_op jit(solution)/shard_map/slice | solution.py:244
  707.1 13.4 %copy.186 = f32[768,4,768]{2,1,0:T(4,128)} copy(f32[768,4,768]{2,0,1:T(8,128)} %bitcast.299) | data formatting | bytes 18874368 | tf_op jit(solution)/shard_map/transpose | solution.py:247
  720.6 12.3 %reshape.281 = f32[1,768,3072]{2,1,0:T(8,128)} reshape(f32[768,4,768]{2,1,0:T(4,128)} %copy.186) | data formatting | bytes 18874368 | tf_op jit(solution)/shard_map/reshape | solution.py:247
  732.8 12.4 %reshape.278 = f32[2,2,768,2,384]{4,3,2,1,0:T(2,128)} reshape(f32[2,1536,768]{2,1,0:T(8,128)} %get-tuple-element.101) | data formatting | bytes 18874368 | tf_op jit(solution)/shard_map/reshape | solution.py:248
  745.3 17.1 %copy.185 = f32[2,2,768,2,384]{4,3,2,1,0:T(2,128)} copy(f32[2,2,768,2,384]{4,1,2,0,3:T(2,128)} %bitcast.300) | data formatting | bytes 18874368 | tf_op jit(solution)/shard_map/transpose | solution.py:249
  762.4 13.2 %reshape.279 = f32[4,1,768,768]{3,2,1,0:T(8,128)} reshape(f32[2,2,768,2,384]{4,3,2,1,0:T(2,128)} %copy.185) | data formatting | bytes 18874368 | tf_op jit(solution)/shard_map/reshape | solution.py:249
  775.6 7.6 slice_bitcast_fusion
  (461 shorter events, 124.0 us)
Async XLA Ops:
  7.2 24.7 %copy-start.15 = (bf16[1,768,768]{2,1,0:T(8,128)(2,1)S(1)}, bf16[1,768,768]{2,1,0:T(8,128)(2,1)}, u32[]{:S(2)}) copy-start(bf16[1,768,768]{2,1,0:T(8,128)(2,1)} %param.17) | copy-start | bytes 3538948
  7.2 335.9 %reduce-scatter.3.cloned.1.call-start = ((), (), s32[]{:S(2)}) async-start(), calls=%async_computation.2 | async-start | bytes 7520256 | tf_op jit(solution)/shard_map/reduce_scatter | solution.py:231
  7.3 21.5 %collective-permute-start.4 = (bf16[1,768,768]{2,1,0:T(8,128)(2,1)}, bf16[1,768,768]{2,1,0:T(8,128)(2,1)S(1)}, u32[]{:S(2)}, u32[]{:S(2)}) collective-permute-start(bf16[1,768,768]{2,1,0:T(8,128)(2,1)} %param.16), channel_id=1, source_target_pairs={{0,16},{16,0},{1,17},{17,1},{2,18},{18,2},{3,19},{19,3},{4,20},{20... | collective-permute-start | bytes 3538952 | tf_op jit(solution)/shard_map/ppermute | solution.py:158
  7.8 49.9 %collective-permute-start.8 = (bf16[1,768,3072]{2,1,0:T(8,128)(2,1)}, bf16[1,768,3072]{2,1,0:T(8,128)(2,1)}, u32[]{:S(2)}, u32[]{:S(2)}) collective-permute-start(bf16[1,768,3072]{2,1,0:T(8,128)(2,1)} %param.20), channel_id=1, source_target_pairs={{0,16},{16,0},{1,17},{17,1},{2,18},{18,2},{3,19},{19,3},{4,20},{20... | collective-permute-start | bytes 14155784 | tf_op jit(solution)/shard_map/ppermute | solution.py:158
  7.9 5.2 collective-permute-start.3
  8.3 10.8 %collective-permute-start.2 = (f32[1,12,12]{2,0,1:T(1,128)}, f32[1,12,12]{2,0,1:T(1,128)}, u32[]{:S(2)}, u32[]{:S(2)}) collective-permute-start(f32[1,12,12]{2,0,1:T(1,128)} %param.25), channel_id=1, source_target_pairs={{0,16},{16,0},{1,17},{17,1},{2,18},{18,2},{3,19},{19,3},{4,20},{20... | collective-permute-start | bytes 1736 | tf_op jit(solution)/shard_map/ppermute | solution.py:158
  8.4 23.5 %collective-permute-start.5 = (bf16[1,768,768]{2,1,0:T(8,128)(2,1)}, bf16[1,768,768]{2,1,0:T(8,128)(2,1)S(1)}, u32[]{:S(2)}, u32[]{:S(2)}) collective-permute-start(bf16[1,768,768]{2,1,0:T(8,128)(2,1)} %param.17), channel_id=1, source_target_pairs={{0,16},{16,0},{1,17},{17,1},{2,18},{18,2},{3,19},{19,3},{4,20},{20... | collective-permute-start | bytes 3538952 | tf_op jit(solution)/shard_map/ppermute | solution.py:158
  13.0 12.6 %collective-permute-start = (f32[1,768]{1,0:T(1,128)}, f32[1,768]{1,0:T(1,128)S(1)}, u32[]{:S(2)}, u32[]{:S(2)}) collective-permute-start(f32[1,768]{1,0:T(1,128)} %param.22), channel_id=1, source_target_pairs={{0,16},{16,0},{1,17},{17,1},{2,18},{18,2},{3,19},{19,3},{4,20},{20... | collective-permute-start | bytes 9224 | tf_op jit(solution)/shard_map/ppermute | solution.py:158
  19.0 8.0 %collective-permute-start.7 = (f32[1,768]{1,0:T(1,128)}, f32[1,768]{1,0:T(1,128)}, u32[]{:S(2)}, u32[]{:S(2)}) collective-permute-start(f32[1,768]{1,0:T(1,128)} %param.23), channel_id=1, source_target_pairs={{0,16},{16,0},{1,17},{17,1},{2,18},{18,2},{3,19},{19,3},{4,20},{20... | collective-permute-start | bytes 9224 | tf_op jit(solution)/shard_map/ppermute | solution.py:158
  26.1 20.3 %collective-permute-start.1 = (bf16[1,768,768]{2,1,0:T(8,128)(2,1)}, bf16[1,768,768]{2,1,0:T(8,128)(2,1)}, u32[]{:S(2)}, u32[]{:S(2)}) collective-permute-start(bf16[1,768,768]{2,1,0:T(8,128)(2,1)} %param.18), channel_id=1, source_target_pairs={{0,16},{16,0},{1,17},{17,1},{2,18},{18,2},{3,19},{19,3},{4,20},{20... | collective-permute-start | bytes 3538952 | tf_op jit(solution)/shard_map/ppermute | solution.py:158
  27.0 37.0 %collective-permute-start.9 = (bf16[1,3072,768]{2,1,0:T(8,128)(2,1)}, bf16[1,3072,768]{2,1,0:T(8,128)(2,1)}, u32[]{:S(2)}, u32[]{:S(2)}) collective-permute-start(bf16[1,3072,768]{2,1,0:T(8,128)(2,1)} %param.21), channel_id=1, source_target_pairs={{0,16},{16,0},{1,17},{17,1},{2,18},{18,2},{3,19},{19,3},{4,20},{20... | collective-permute-start | bytes 14155784 | tf_op jit(solution)/shard_map/ppermute | solution.py:158
  28.8 25.8 %collective-permute-start.6 = (bf16[1,768,768]{2,1,0:T(8,128)(2,1)}, bf16[1,768,768]{2,1,0:T(8,128)(2,1)}, u32[]{:S(2)}, u32[]{:S(2)}) collective-permute-start(bf16[1,768,768]{2,1,0:T(8,128)(2,1)} %param.19), channel_id=1, source_target_pairs={{0,16},{16,0},{1,17},{17,1},{2,18},{18,2},{3,19},{19,3},{4,20},{20... | collective-permute-start | bytes 3538952 | tf_op jit(solution)/shard_map/ppermute | solution.py:158
  53.6 121.6 %collective-permute-start.20 = (bf16[256,768]{0,1:T(8,128)(2,1)}, bf16[256,768]{0,1:T(8,128)(2,1)}, u32[]{:S(2)}, u32[]{:S(2)}) collective-permute-start(bf16[256,768]{0,1:T(8,128)(2,1)} %bitcast.10), channel_id=1, source_target_pairs={{0,16},{16,0},{1,17},{17,1},{2,18},{18,2},{3,19},{19,3},{4,20},{20... | collective-permute-start | bytes 1179656 | tf_op jit(solution)/shard_map/ppermute | solution.py:158
  80.8 9.0 %slice-start.6 = ((s8[4718592]{0:T(1024)(128)(4,1)}), s8[4194304]{0:T(1024)(128)(4,1)S(1)}, s32[]{:S(2)}) async-start(s8[4718592]{0:T(1024)(128)(4,1)} %bitcast.340), calls=%async_computation.11 | async-start | bytes 8388608
  94.1 11.1 %copy-start.44 = (bf16[256,3072]{1,0:T(8,128)(2,1)}, bf16[256,3072]{1,0:T(8,128)(2,1)S(1)}, u32[]{:S(2)}) copy-start(bf16[256,3072]{1,0:T(8,128)(2,1)S(1)} %get-tuple-element.167) | copy-start | bytes 4718596
  118.8 14.6 %copy-start.27 = (bf16[12,64,256]{2,1,0:T(8,128)(2,1)}, bf16[12,64,256]{2,1,0:T(8,128)(2,1)S(1)}, u32[]{:S(2)}) copy-start(bf16[12,64,256]{2,1,0:T(8,128)(2,1)S(1)} %convolution_convert_fusion.14) | copy-start | bytes 1179652
  139.2 7.9 %copy-start.8 = (bf16[256,768]{1,0:T(8,128)(2,1)}, bf16[256,768]{1,0:T(8,128)(2,1)S(1)}, u32[]{:S(2)}) copy-start(bf16[256,768]{1,0:T(8,128)(2,1)S(1)} %get-tuple-element.90) | copy-start | bytes 1179652
  169.2 11.9 %collective-permute-start.15 = (bf16[256,1536]{1,0:T(8,128)(2,1)S(1)}, bf16[256,1536]{1,0:T(8,128)(2,1)S(1)}, u32[]{:S(2)}, u32[]{:S(2)}) collective-permute-start(bf16[256,1536]{1,0:T(8,128)(2,1)S(1)} %copy-done.64), channel_id=1, source_target_pairs={{0,16},{16,0},{1,17},{17,1},{2,18},{18,2},{3,19},{19,3},{4,20},{20... | collective-permute-start | bytes 2359304 | tf_op jit(solution)/shard_map/ppermute | solution.py:158
  173.5 5.0 collective-permute-start.16
  174.7 1.5 collective-permute-start.21
  174.7 1.8 collective-permute-start.18
  175.3 7.3 collective-permute-start.12
  176.2 4.9 collective-permute-start.14
  176.6 2.9 collective-permute-start.19
  178.6 1.9 collective-permute-start.17
  179.5 3.1 collective-permute-start.13
  189.8 308.4 %reduce-scatter.5.cloned.1.call-start = ((), (), s32[]{:S(2)}) async-start(), calls=%async_computation.3 | async-start | bytes 7520256 | tf_op jit(solution)/shard_map/reduce_scatter | solution.py:231
  190.1 7.7 collective-permute-start.26
  191.7 4.0 collective-permute-start.31
  193.1 2.9 collective-permute-start.29
  194.9 6.7 collective-permute-start.25
  195.3 2.2 collective-permute-start.28
  195.7 5.3 collective-permute-start.30
  196.0 7.0 collective-permute-start.22
  197.5 4.0 collective-permute-start.24
  197.8 2.2 collective-permute-start.27
  200.0 3.0 collective-permute-start.23
  210.3 297.0 %copy-start.110 = (f32[256]{0:T(256)S(1)}, f32[256]{0:T(256)}, u32[]{:S(2)}) copy-start(f32[256]{0:T(256)} %get-tuple-element.125) | copy-start | bytes 3076
  210.3 460.3 %all-gather.3.cloned.1.call-start = ((), (), s32[]{:S(2)}) async-start(), calls=%async_computation.4 | async-start | bytes 15040512 | tf_op jit(solution)/shard_map/all_gather | solution.py:237
  499.4 1.9 collective-permute-start.32
  504.6 1.4 collective-permute-start.34
  510.3 105.9 %collective-permute-start.10 = (bf16[256,768]{1,0:T(8,128)(2,1)}, bf16[256,768]{1,0:T(8,128)(2,1)}, u32[]{:S(2)}, u32[]{:S(2)}) collective-permute-start(bf16[256,768]{1,0:T(8,128)(2,1)} %broadcast_select_fusion.42), channel_id=1, source_target_pairs={{0,16},{16,0},{1,17},{17,1},{2,18},{18,2},{3,19},{19,3},{4,20},{20... | collective-permute-start | bytes 1179656 | tf_op jit(solution)/shard_map/ppermute | solution.py:158
  520.6 15.8 %copy-start.108 = (f32[768]{0:T(1024)S(1)}, f32[768]{0:T(1024)}, u32[]{:S(2)}) copy-start(f32[768]{0:T(1024)} %get-tuple-element.69) | copy-start | bytes 9220
  539.2 10.1 %copy-start.3 = (f32[12,256,256]{2,1,0:T(8,128)S(1)}, f32[12,256,256]{2,1,0:T(8,128)}, u32[]{:S(2)}) copy-start(f32[12,256,256]{2,1,0:T(8,128)} %copy-done.2) | copy-start | bytes 9437188
  559.0 57.3 %copy-start.51 = (bf16[256,768]{1,0:T(8,128)(2,1)S(1)}, bf16[256,768]{1,0:T(8,128)(2,1)}, u32[]{:S(2)}) copy-start(bf16[256,768]{1,0:T(8,128)(2,1)} %get-tuple-element.123) | copy-start | bytes 1179652
  566.2 3.3 collective-permute-start.33
  567.4 51.0 %copy-start.9 = (bf16[256,768]{1,0:T(8,128)(2,1)S(1)}, bf16[256,768]{1,0:T(8,128)(2,1)}, u32[]{:S(2)}) copy-start(bf16[256,768]{1,0:T(8,128)(2,1)} %copy-done.8) | copy-start | bytes 1179652
  569.5 48.8 %collective-permute-start.11 = (bf16[256,768]{1,0:T(8,128)(2,1)S(1)}, bf16[256,768]{1,0:T(8,128)(2,1)S(1)}, u32[]{:S(2)}, u32[]{:S(2)}) collective-permute-start(bf16[256,768]{1,0:T(8,128)(2,1)S(1)} %get-tuple-element.85), channel_id=1, source_target_pairs={{0,16},{16,0},{1,17},{17,1},{2,18},{18,2},{3,19},{19,3},{4,20},{20... | collective-permute-start | bytes 1179656 | tf_op jit(solution)/shard_map/ppermute | solution.py:158
  (122 other events, 467.8 us)
Sparse Core Ops, SparseCore 0:
  190.0 153.1 reduce-scatter.2
  349.0 149.2 reduce-scatter.4
  503.5 167.0 all-gather.2
where the time goes:
time: 800 us; the launch traced here: 790 us
  waiting for transfers between devices  351 us (44%)
  matrix products  167 us (21%)
  local copies, waits for them, and re-layouts  160 us (20%)
  blocking collectives  42.1 us (5%)
  other arithmetic  41.5 us (5%)
  between operations  17.4 us (2%)
  starting transfers between devices  10.8 us (1%)
    reduce_scatter x2, waiting for transfers between devices, local(): lax.psum_scatter(grad, 'dp', scatter_dimension=0, tiled=True)  288 us
    dot_general x36, matrix products, dot(): lax.dot_general(a, b, ((dims[0], dims[1]), ((), ())), preferred_element_t...  74.7 us
    all_gather x1, waiting for transfers between devices, local(): whole = lax.all_gather(halves, 'dp', axis=0)  51.2 us
    psum x1, blocking collectives, local(): tail = lax.psum(tail, 'dp')  42.1 us
    dot_general x8, matrix products, mix_heads(): return jnp.einsum('gh,hij->gij', mix, values, precision=lax.Precision.HIGH)  38.5 us
    slice x1, local copies, waits for them, and re-layouts, local(): w_out_grad = whole[:, :count].reshape(1, hidden, width)  20.8 us
    dot_general x2, matrix products, backward_attention(): jnp.einsum('gij,hij->gh', grad_logits, scores, precision=lax.Precision.HIGH)  19.8 us
    dot_general x2, matrix products, backward_attention(): jnp.einsum('gij,hij->gh', grad_weights, probs, precision=lax.Precision.HIGH)  17.7 us
  transfers between devices with their start and end apart: 38, of which 9 were waited for; matrix products, arithmetic and copies ran while one was open for 30% of the time, Pallas kernels for 0%

commit v1 on v0

--- a/solution.py
+++ b/solution.py
@@ -251,7 +251,8 @@
     total_small = jnp.where(is_first, both, both[::-1])
     mine_small = total_small[0] + swap(total_small[1])
     tail = jnp.concatenate([mine_small, jnp.sum(valid)[None] + swap(jnp.sum(valid)[None])])
-    tail = lax.psum(tail, "dp")
+    shards_2 = lax.all_gather(tail, "dp", axis=0, tiled=False)
+    tail = shards_2.sum(axis=0)
     heads = mix_pre.shape[1]
     square = heads * heads
     at = 2 * width

time: 800 us -> 910 us (1.14)
  waiting for transfers between devices: 351 us -> 498 us
  blocking collectives: 42.1 us -> 0 us
    all_gather x1, waiting for transfers between devices: 51.2 us -> 161 us  [local(): whole = lax.all_gather(halves, 'dp', axis=0)]
    unnamed x3 -> x5, waiting for transfers between devices: 0.05 us -> 97 us
    reduce_scatter x2, waiting for transfers between devices: 288 us -> 231 us  [local(): lax.psum_scatter(grad, 'dp', scatter_dimension=0, tiled=True)]
    psum x1 -> x0, blocking collectives: 42.1 us -> none  [local(): tail = lax.psum(tail, 'dp')]
  transfers between devices with their start and end apart: 38 -> 39, of which waited for: 9 -> 8; matrix products, arithmetic and copies ran while one was open for 30% -> 27% of each run, Pallas kernels for 0% -> 0%
where the time goes in v1:
time: 910 us; the launch traced here: 900 us
  waiting for transfers between devices  498 us (55%)
  matrix products  167 us (18%)
  local copies, waits for them, and re-layouts  163 us (18%)
  other arithmetic  42.8 us (5%)
  between operations  18.3 us (2%)
  starting transfers between devices  11.4 us (1%)
    reduce_scatter x2, waiting for transfers between devices, local(): lax.psum_scatter(grad, 'dp', scatter_dimension=0, tiled=True)  231 us
    all_gather x1, waiting for transfers between devices, local(): whole = lax.all_gather(halves, 'dp', axis=0)  161 us
    unnamed x5, waiting for transfers between devices  97 us
    dot_general x36, matrix products, dot(): lax.dot_general(a, b, ((dims[0], dims[1]), ((), ())), preferred_element_t...  74.7 us
    dot_general x8, matrix products, mix_heads(): return jnp.einsum('gh,hij->gij', mix, values, precision=lax.Precision.HIGH)  38.5 us
    slice x1, local copies, waits for them, and re-layouts, local(): w_out_grad = whole[:, :count].reshape(1, hidden, width)  20.8 us
    dot_general x2, matrix products, backward_attention(): jnp.einsum('gij,hij->gh', grad_logits, scores, precision=lax.Precision.HIGH)  19.5 us
  transfers between devices with their start and end apart: 39, of which 8 were waited for; matrix products, arithmetic and copies ran while one was open for 27% of the time, Pallas kernels for 0%

profile of v1, /device:TPU:0, one launch (start us, length us, event | category | flops | bytes accessed | tf_op | source)
XLA Modules:
  0.0 899.7 jit_solution(12333672199547816501)
XLA Ops:
  13.0 6.0 collective-permute-done.2
  28.9 3.0 convolution_convert_fusion.22
  38.2 4.2 select_reduce_fusion.1
  42.4 2.1 copy-done.4
  44.5 1.9 fusion.45
  47.3 4.8 fusion.204
  54.6 2.3 multiply_reduce_fusion.13
  57.7 6.3 multiply_convert_fusion.1
  64.0 2.5 fusion.138
  76.6 4.2 select_reduce_fusion
  80.8 2.4 fusion.47
  83.2 3.1 fusion.199
  87.1 2.8 multiply_reduce_fusion.12
  90.1 4.2 multiply_convert_fusion
  94.4 5.9 fusion.38
  100.3 5.2 multiply_reduce_fusion.5
  105.5 5.8 fusion.246
  112.0 2.6 convolution_convert_fusion.15
  116.6 2.5 convolution_convert_fusion.14
  121.1 6.7 multiply_reduce_fusion.1
  127.8 4.3 fusion.74
  133.5 2.1 fusion.90
  139.6 3.1 fusion.41
  144.7 2.5 multiply_reduce_fusion.6
  152.5 2.5 convolution_convert_fusion.12
  156.7 7.0 multiply_reduce_fusion
  163.7 4.3 fusion.75
  171.6 2.1 fusion.131
  182.8 2.8 fusion.49
  203.0 2.8 fusion.48
  212.2 8.6 fusion.104
  222.1 9.8 %fusion.113 = f32[12,12]{1,0:T(8,128)} fusion(f32[12,256,256]{2,1,0:T(8,128)S(1)} %convolution_multiply_fusion, f32[12,256,256]{2,0,1:T(8,128)} %copy-done.122, f32[12,256]{0,1:T(8,128)} %copy-done.124, f32[12,256,256]{2,0,1:T(8,128)} %copy-done.6, f32[12,256]{0,1:T(8,128)} %copy-done.86, f32[12,256]{0,1:T(8,128)} %copy-done.71, ...), kind=kOutput, calls=%fused_computation.179 | convolution fusion | flops 60555264 | bytes 9540160 | tf_op jit(solution)/shard_map/gij,hij->gh/dot_general | solution.py:116
  237.7 2.7 concatenate.118
  240.4 8.7 fusion.107
  250.5 9.7 %fusion.110 = f32[12,12]{1,0:T(8,128)} fusion(f32[12,256,256]{2,1,0:T(8,128)S(1)} %copy-done.3, f32[12,256,256]{2,0,1:T(8,128)} %copy-done.123, f32[12,256]{0,1:T(8,128)} %copy-done.125, f32[12,256,256]{2,0,1:T(8,128)} %copy-done.4, f32[12,256]{0,1:T(8,128)} %copy-done.84, f32[12,256]{0,1:T(8,128)} %copy-done.69, pred[256,256]{1,0:T(8,128)(4,1)} %iota_compare_fusion), kind=kOutput, calls=%fused_computation.178 | convolution fusion | flops 60555264 | bytes 9540160 | tf_op jit(solution)/shard_map/gij,hij->gh/dot_general | solution.py:116
  264.2 2.7 concatenate.117
  267.3 76.0 %reduce-scatter.3.cloned.1.call-done = bf16[288,768]{1,0:T(8,128)(2,1)} async-done(((bf16[4608,768]{1,0:T(8,128)(2,1)}), bf16[288,768]{1,0:T(8,128)(2,1)}) %reduce-scatter.3.cloned.1.call-update) | async-done | bytes 442384 | tf_op jit(solution)/shard_map/reduce_scatter | solution.py:231
  343.3 155.1 %reduce-scatter.5.cloned.1.call-done = bf16[288,768]{1,0:T(8,128)(2,1)} async-done(((bf16[4608,768]{1,0:T(8,128)(2,1)}), bf16[288,768]{1,0:T(8,128)(2,1)}) %reduce-scatter.5.cloned.1.call-update) | async-done | bytes 442384 | tf_op jit(solution)/shard_map/reduce_scatter | solution.py:231
  514.0 96.9 %all-reduce.3.cloned.1.call-done = f32[29248]{0:T(1024)} async-done(((f32[29248]{0:T(1024)}), f32[29248]{0:T(1024)}) %all-reduce.3.cloned.1.call-update) | async-done | bytes 117008
  619.5 160.8 %all-gather.4.cloned.1.call-done = bf16[9216,768]{1,0:T(8,128)(2,1)} async-done(((bf16[576,768]{1,0:T(8,128)(2,1)}), bf16[9216,768]{1,0:T(8,128)(2,1)}) %all-gather.4.cloned.1.call-update) | async-done | bytes 14155792 | tf_op jit(solution)/shard_map/all_gather | solution.py:237
  780.2 15.7 %copy.184 = f32[16,2,288,768]{3,2,0,1:T(8,128)} copy(bf16[16,2,288,768]{3,2,1,0:T(8,128)(2,1)} %bitcast.302) | data formatting | bytes 42467328 | tf_op jit(solution)/shard_map/convert_element_type | solution.py:240
  795.9 20.8 %fusion.250 = (f32[2,1536,768]{2,1,0:T(8,128)}, f32[2,1536,768]{2,1,0:T(8,128)}, f32[2,1536,768]{2,1,0:T(8,128)}) fusion(f32[2,4608,768]{2,1,0:T(8,128)} %bitcast.299), kind=kLoop, calls=%fused_computation.396 | loop fusion | bytes 56623104 | tf_op jit(solution)/shard_map/slice | solution.py:244
  816.7 13.5 %copy.186 = f32[768,4,768]{2,1,0:T(4,128)} copy(f32[768,4,768]{2,0,1:T(8,128)} %bitcast.300) | data formatting | bytes 18874368 | tf_op jit(solution)/shard_map/transpose | solution.py:247
  830.1 12.3 %reshape.281 = f32[1,768,3072]{2,1,0:T(8,128)} reshape(f32[768,4,768]{2,1,0:T(4,128)} %copy.186) | data formatting | bytes 18874368 | tf_op jit(solution)/shard_map/reshape | solution.py:247
  842.4 12.4 %reshape.278 = f32[2,2,768,2,384]{4,3,2,1,0:T(2,128)} reshape(f32[2,1536,768]{2,1,0:T(8,128)} %get-tuple-element.101) | data formatting | bytes 18874368 | tf_op jit(solution)/shard_map/reshape | solution.py:248
  854.8 17.1 %copy.185 = f32[2,2,768,2,384]{4,3,2,1,0:T(2,128)} copy(f32[2,2,768,2,384]{4,1,2,0,3:T(2,128)} %bitcast.301) | data formatting | bytes 18874368 | tf_op jit(solution)/shard_map/transpose | solution.py:249
  871.9 13.2 %reshape.279 = f32[4,1,768,768]{3,2,1,0:T(8,128)} reshape(f32[2,2,768,2,384]{4,3,2,1,0:T(2,128)} %copy.185) | data formatting | bytes 18874368 | tf_op jit(solution)/shard_map/reshape | solution.py:249
  885.2 7.6 slice_bitcast_fusion
  (475 shorter events, 126.1 us)
Async XLA Ops:
  7.2 24.7 %copy-start.15 = (bf16[1,768,768]{2,1,0:T(8,128)(2,1)S(1)}, bf16[1,768,768]{2,1,0:T(8,128)(2,1)}, u32[]{:S(2)}) copy-start(bf16[1,768,768]{2,1,0:T(8,128)(2,1)} %param.17) | copy-start | bytes 3538948
  7.2 336.1 %reduce-scatter.3.cloned.1.call-start = ((), (), s32[]{:S(2)}) async-start(), calls=%async_computation.2 | async-start | bytes 7520256 | tf_op jit(solution)/shard_map/reduce_scatter | solution.py:231
  7.3 21.5 %collective-permute-start.4 = (bf16[1,768,768]{2,1,0:T(8,128)(2,1)}, bf16[1,768,768]{2,1,0:T(8,128)(2,1)S(1)}, u32[]{:S(2)}, u32[]{:S(2)}) collective-permute-start(bf16[1,768,768]{2,1,0:T(8,128)(2,1)} %param.16), channel_id=1, source_target_pairs={{0,16},{16,0},{1,17},{17,1},{2,18},{18,2},{3,19},{19,3},{4,20},{20... | collective-permute-start | bytes 3538952 | tf_op jit(solution)/shard_map/ppermute | solution.py:158
  7.8 49.9 %collective-permute-start.8 = (bf16[1,768,3072]{2,1,0:T(8,128)(2,1)}, bf16[1,768,3072]{2,1,0:T(8,128)(2,1)}, u32[]{:S(2)}, u32[]{:S(2)}) collective-permute-start(bf16[1,768,3072]{2,1,0:T(8,128)(2,1)} %param.20), channel_id=1, source_target_pairs={{0,16},{16,0},{1,17},{17,1},{2,18},{18,2},{3,19},{19,3},{4,20},{20... | collective-permute-start | bytes 14155784 | tf_op jit(solution)/shard_map/ppermute | solution.py:158
  7.9 5.1 collective-permute-start.3
  8.3 10.8 %collective-permute-start.2 = (f32[1,12,12]{2,0,1:T(1,128)}, f32[1,12,12]{2,0,1:T(1,128)}, u32[]{:S(2)}, u32[]{:S(2)}) collective-permute-start(f32[1,12,12]{2,0,1:T(1,128)} %param.25), channel_id=1, source_target_pairs={{0,16},{16,0},{1,17},{17,1},{2,18},{18,2},{3,19},{19,3},{4,20},{20... | collective-permute-start | bytes 1736 | tf_op jit(solution)/shard_map/ppermute | solution.py:158
  8.4 23.5 %collective-permute-start.5 = (bf16[1,768,768]{2,1,0:T(8,128)(2,1)}, bf16[1,768,768]{2,1,0:T(8,128)(2,1)S(1)}, u32[]{:S(2)}, u32[]{:S(2)}) collective-permute-start(bf16[1,768,768]{2,1,0:T(8,128)(2,1)} %param.17), channel_id=1, source_target_pairs={{0,16},{16,0},{1,17},{17,1},{2,18},{18,2},{3,19},{19,3},{4,20},{20... | collective-permute-start | bytes 3538952 | tf_op jit(solution)/shard_map/ppermute | solution.py:158
  13.0 12.6 %collective-permute-start = (f32[1,768]{1,0:T(1,128)}, f32[1,768]{1,0:T(1,128)S(1)}, u32[]{:S(2)}, u32[]{:S(2)}) collective-permute-start(f32[1,768]{1,0:T(1,128)} %param.22), channel_id=1, source_target_pairs={{0,16},{16,0},{1,17},{17,1},{2,18},{18,2},{3,19},{19,3},{4,20},{20... | collective-permute-start | bytes 9224 | tf_op jit(solution)/shard_map/ppermute | solution.py:158
  19.0 8.0 collective-permute-start.7
  26.1 20.3 %collective-permute-start.1 = (bf16[1,768,768]{2,1,0:T(8,128)(2,1)}, bf16[1,768,768]{2,1,0:T(8,128)(2,1)}, u32[]{:S(2)}, u32[]{:S(2)}) collective-permute-start(bf16[1,768,768]{2,1,0:T(8,128)(2,1)} %param.18), channel_id=1, source_target_pairs={{0,16},{16,0},{1,17},{17,1},{2,18},{18,2},{3,19},{19,3},{4,20},{20... | collective-permute-start | bytes 3538952 | tf_op jit(solution)/shard_map/ppermute | solution.py:158
  27.0 37.0 %collective-permute-start.9 = (bf16[1,3072,768]{2,1,0:T(8,128)(2,1)}, bf16[1,3072,768]{2,1,0:T(8,128)(2,1)}, u32[]{:S(2)}, u32[]{:S(2)}) collective-permute-start(bf16[1,3072,768]{2,1,0:T(8,128)(2,1)} %param.21), channel_id=1, source_target_pairs={{0,16},{16,0},{1,17},{17,1},{2,18},{18,2},{3,19},{19,3},{4,20},{20... | collective-permute-start | bytes 14155784 | tf_op jit(solution)/shard_map/ppermute | solution.py:158
  28.8 25.8 %collective-permute-start.6 = (bf16[1,768,768]{2,1,0:T(8,128)(2,1)}, bf16[1,768,768]{2,1,0:T(8,128)(2,1)}, u32[]{:S(2)}, u32[]{:S(2)}) collective-permute-start(bf16[1,768,768]{2,1,0:T(8,128)(2,1)} %param.19), channel_id=1, source_target_pairs={{0,16},{16,0},{1,17},{17,1},{2,18},{18,2},{3,19},{19,3},{4,20},{20... | collective-permute-start | bytes 3538952 | tf_op jit(solution)/shard_map/ppermute | solution.py:158
  53.6 121.9 %collective-permute-start.20 = (bf16[256,768]{0,1:T(8,128)(2,1)}, bf16[256,768]{0,1:T(8,128)(2,1)}, u32[]{:S(2)}, u32[]{:S(2)}) collective-permute-start(bf16[256,768]{0,1:T(8,128)(2,1)} %bitcast.10), channel_id=1, source_target_pairs={{0,16},{16,0},{1,17},{17,1},{2,18},{18,2},{3,19},{19,3},{4,20},{20... | collective-permute-start | bytes 1179656 | tf_op jit(solution)/shard_map/ppermute | solution.py:158
  80.8 9.3 %slice-start.6 = ((s8[4718592]{0:T(1024)(128)(4,1)}), s8[4194304]{0:T(1024)(128)(4,1)S(1)}, s32[]{:S(2)}) async-start(s8[4718592]{0:T(1024)(128)(4,1)} %bitcast.341), calls=%async_computation.12 | async-start | bytes 8388608
  94.4 11.1 %copy-start.47 = (bf16[256,3072]{1,0:T(8,128)(2,1)}, bf16[256,3072]{1,0:T(8,128)(2,1)S(1)}, u32[]{:S(2)}) copy-start(bf16[256,3072]{1,0:T(8,128)(2,1)S(1)} %get-tuple-element.167) | copy-start | bytes 4718596
  119.1 14.3 %copy-start.27 = (bf16[12,64,256]{2,1,0:T(8,128)(2,1)}, bf16[12,64,256]{2,1,0:T(8,128)(2,1)S(1)}, u32[]{:S(2)}) copy-start(bf16[12,64,256]{2,1,0:T(8,128)(2,1)S(1)} %convolution_convert_fusion.14) | copy-start | bytes 1179652
  139.3 7.9 copy-start.8
  169.4 11.9 %collective-permute-start.15 = (bf16[256,1536]{1,0:T(8,128)(2,1)S(1)}, bf16[256,1536]{1,0:T(8,128)(2,1)S(1)}, u32[]{:S(2)}, u32[]{:S(2)}) collective-permute-start(bf16[256,1536]{1,0:T(8,128)(2,1)S(1)} %copy-done.67), channel_id=1, source_target_pairs={{0,16},{16,0},{1,17},{17,1},{2,18},{18,2},{3,19},{19,3},{4,20},{20... | collective-permute-start | bytes 2359304 | tf_op jit(solution)/shard_map/ppermute | solution.py:158
  173.7 5.0 collective-permute-start.16
  174.9 1.5 collective-permute-start.21
  174.9 1.8 collective-permute-start.18
  175.5 7.3 collective-permute-start.12
  176.4 4.9 collective-permute-start.14
  176.8 2.9 collective-permute-start.19
  178.8 1.9 collective-permute-start.17
  179.7 3.1 collective-permute-start.13
  190.1 308.4 %reduce-scatter.5.cloned.1.call-start = ((), (), s32[]{:S(2)}) async-start(), calls=%async_computation.3 | async-start | bytes 7520256 | tf_op jit(solution)/shard_map/reduce_scatter | solution.py:231
  190.1 7.7 collective-permute-start.26
  191.7 4.0 collective-permute-start.31
  193.1 2.9 collective-permute-start.29
  194.9 6.7 collective-permute-start.25
  195.3 2.2 collective-permute-start.28
  195.7 5.3 collective-permute-start.30
  196.0 7.0 collective-permute-start.22
  197.5 4.1 collective-permute-start.24
  197.8 2.2 collective-permute-start.27
  200.0 3.0 collective-permute-start.23
  210.3 400.6 %all-reduce.3.cloned.1.call-start = ((), (), s32[]{:S(2)}) async-start(), calls=%async_computation.5 | async-start | bytes 237568
  222.1 15.6 %copy-start.112 = (f32[768]{0:T(1024)S(1)}, f32[768]{0:T(1024)}, u32[]{:S(2)}) copy-start(f32[768]{0:T(1024)} %get-tuple-element.69) | copy-start | bytes 9220
  240.4 10.1 %copy-start.3 = (f32[12,256,256]{2,1,0:T(8,128)S(1)}, f32[12,256,256]{2,1,0:T(8,128)}, u32[]{:S(2)}) copy-start(f32[12,256,256]{2,1,0:T(8,128)} %copy-done.2) | copy-start | bytes 9437188
  267.3 242.9 %copy-start.54 = (bf16[256,768]{1,0:T(8,128)(2,1)S(1)}, bf16[256,768]{1,0:T(8,128)(2,1)}, u32[]{:S(2)}) copy-start(bf16[256,768]{1,0:T(8,128)(2,1)} %get-tuple-element.123) | copy-start | bytes 1179652
  500.3 7.7 collective-permute-start.32
  500.4 5.0 collective-permute-start.33
  502.2 1.9 collective-permute-start.34
  507.7 272.5 %all-gather.4.cloned.1.call-start = ((), (), s32[]{:S(2)}) async-start(), calls=%async_computation.4 | async-start | bytes 15040512 | tf_op jit(solution)/shard_map/all_gather | solution.py:237
  511.0 105.4 %collective-permute-start.10 = (bf16[256,768]{1,0:T(8,128)(2,1)}, bf16[256,768]{1,0:T(8,128)(2,1)}, u32[]{:S(2)}, u32[]{:S(2)}) collective-permute-start(bf16[256,768]{1,0:T(8,128)(2,1)} %broadcast_select_fusion.42), channel_id=1, source_target_pairs={{0,16},{16,0},{1,17},{17,1},{2,18},{18,2},{3,19},{19,3},{4,20},{20... | collective-permute-start | bytes 1179656 | tf_op jit(solution)/shard_map/ppermute | solution.py:158
  514.0 104.5 %collective-permute-start.11 = (bf16[256,768]{1,0:T(8,128)(2,1)}, bf16[256,768]{1,0:T(8,128)(2,1)S(1)}, u32[]{:S(2)}, u32[]{:S(2)}) collective-permute-start(bf16[256,768]{1,0:T(8,128)(2,1)} %get-tuple-element.85), channel_id=1, source_target_pairs={{0,16},{16,0},{1,17},{17,1},{2,18},{18,2},{3,19},{19,3},{4,20},{20... | collective-permute-start | bytes 1179656 | tf_op jit(solution)/shard_map/ppermute | solution.py:158
  885.2 7.6 copy-start.1
  (127 other events, 495.7 us)
Sparse Core Ops, SparseCore 0:
  190.2 153.1 reduce-scatter.2
  349.2 149.1 reduce-scatter.4
  507.8 103.0 all-reduce.2
  614.1 166.0 all-gather.3
